TPU v7x, 256 devices: a whole 4x4x8 slice. The times are simulated.
256 devices in a mesh: rows: 16 (over x_hi, y, core), modes: 16 (over x_lo, z).
Axes of the slice: x: 4 (x_hi: 2, x_lo: 2; x = x_hi * 2 + x_lo), y: 4, z: 8, core: 2. Of those that a mesh axis runs over, the one named last changes fastest.
Arguments:
- transfer: float32 [16384, 16384], P('rows', 'modes'), may hold values from -1 to 1
- observed: float32 [256, 16384], P('modes', 'rows'), may hold values from -6 to 6
- start: float32 [256, 16384], P('rows', 'modes'), may hold values from -6 to 6
- probe: bfloat16 [256, 16384], P(('rows', 'modes')), may hold values from -6 to 6
- w_first: bfloat16 [9, 48, 2], replicated, may hold values from -1.5 to 1.5
- w_mid: bfloat16 [9, 48, 48], replicated, may hold values from -0.3125 to 0.3125
- w_last: bfloat16 [9, 1, 48], replicated, may hold values from -0.3125 to 0.3125
Outputs:
- recovered: float32 [256, 16384], P(('rows', 'modes'))
All inputs are finite; a program needn't handle non-finite values.
Results may differ from a plain program's by a relative error of at most 0.0049.
Values sent between devices are 32-bit elements; how exact they have to be, the bound alone decides.
No kernel may reach another device: no remote copies, remote signals or barrier semaphores. Data moves between devices by JAX's collectives and lax.ppermute only.
A program may use at most 128 MiB of HBM per device.

v0:
```python
import jax
import jax.numpy as jnp
from jax import lax
from jax.sharding import PartitionSpec as P

IMG = 128
ITERS = 2
PIX = 16384


def conv_layer(weights, feature):
    in_chan, extent_rows, extent_cols = feature.shape
    out_chan = weights.shape[1]
    padded = jnp.pad(feature, ((0, 0), (1, 1), (1, 1)))
    if out_chan == 1:
        taps_flat = weights[:, 0, :]
        products = jnp.dot(
            taps_flat,
            feature.reshape(in_chan, extent_rows * extent_cols),
            preferred_element_type=jnp.float32,
        )
        products = jnp.pad(products.reshape(9, extent_rows, extent_cols), ((0, 0), (1, 1), (1, 1)))
        summed = jnp.zeros((extent_rows, extent_cols), jnp.float32)
        for offset in range(9):
            row_shift = offset // 3
            col_shift = offset % 3
            summed = (
                summed
                + products[
                    offset, row_shift : row_shift + extent_rows, col_shift : col_shift + extent_cols
                ]
            )
        return summed.reshape(1, extent_rows, extent_cols)
    windows = []
    for offset in range(9):
        row_shift = offset // 3
        col_shift = offset % 3
        windows.append(
            padded[:, row_shift : row_shift + extent_rows, col_shift : col_shift + extent_cols]
        )
    columns = jnp.concatenate(windows, axis=0).reshape(9 * in_chan, extent_rows * extent_cols)
    weight_flat = jnp.transpose(weights, (1, 0, 2)).reshape(out_chan, 9 * in_chan)
    summed = jnp.dot(weight_flat, columns, preferred_element_type=jnp.float32)
    return summed.reshape(out_chan, extent_rows, extent_cols)


def silu_slope(values):
    logistic = jax.nn.sigmoid(values)
    return logistic * (1.0 + values * (1.0 - logistic))


def denoise(bundle, w_first, w_mid, w_last):
    pushed_one, levels_one, probe_one = bundle
    picture = pushed_one.reshape(IMG, IMG)
    stacked = jnp.stack([picture, jnp.zeros_like(picture) + levels_one]).astype(jnp.bfloat16)
    first_pre = conv_layer(w_first, stacked)
    first_tan = conv_layer(w_first[:, :, 0:1], probe_one.reshape(1, IMG, IMG))
    active_one = jax.nn.silu(first_pre).astype(jnp.bfloat16)
    tan_one = (silu_slope(first_pre) * first_tan).astype(jnp.bfloat16)
    second_pre = conv_layer(w_mid, active_one)
    second_tan = conv_layer(w_mid, tan_one)
    active_two = jax.nn.silu(second_pre).astype(jnp.bfloat16)
    tan_two = (silu_slope(second_pre) * second_tan).astype(jnp.bfloat16)
    out_pre = conv_layer(w_last, active_two).reshape(-1)
    out_tan = conv_layer(w_last, tan_two).reshape(-1)
    denoised = pushed_one - out_pre
    probe_vals = probe_one.astype(jnp.float32)
    spread = jnp.mean(probe_vals * (probe_vals - out_tan))
    return (denoised, spread)


def body(transfer, observed, start, probe, w_first, w_mid, w_last):
    frames_dev = probe.shape[0]
    offset_frame = (
        lax.axis_index("rows") * lax.axis_size("modes") + lax.axis_index("modes")
    ) * frames_dev
    trace = lax.psum(jnp.sum(transfer * transfer), ("rows", "modes"))
    estimate = start
    recovered = None
    for iteration in range(ITERS):
        partial_value = lax.dot_general(
            lax.all_gather(estimate, "rows", axis=0, tiled=True),
            transfer,
            (((1,), (1,)), ((), ())),
            precision=lax.Precision.HIGHEST,
            preferred_element_type=jnp.float32,
        )
        fitted = lax.psum_scatter(partial_value, "modes", scatter_dimension=0, tiled=True)
        misfit_all = lax.all_gather(observed - fitted, "modes", axis=0, tiled=True)
        square_part = jnp.sum(misfit_all * misfit_all, axis=1, keepdims=True)
        squares_all = lax.psum(square_part[:, 0], "rows")
        squares = lax.dynamic_slice_in_dim(squares_all, offset_frame, frames_dev)
        back_sum = lax.psum_scatter(
            jnp.dot(
                misfit_all,
                transfer,
                precision=lax.Precision.HIGHEST,
                preferred_element_type=jnp.float32,
            ),
            "rows",
            scatter_dimension=0,
            tiled=True,
        )
        pushed_rows = estimate + PIX / trace * back_sum
        pushed = lax.all_to_all(pushed_rows, "modes", split_axis=0, concat_axis=1, tiled=True)
        levels = jnp.sqrt(squares / trace)
        denoised, spread = lax.map(
            lambda bundle: denoise(bundle, w_first, w_mid, w_last), (pushed, levels, probe)
        )
        onsager = denoised - spread[:, None] * pushed
        gains = jnp.sum(denoised * onsager, axis=1) / (jnp.sum(onsager * onsager, axis=1) + 1e-06)
        recovered = gains[:, None] * onsager
        if iteration + 1 < ITERS:
            estimate = lax.all_to_all(recovered, "modes", split_axis=1, concat_axis=0, tiled=True)
    return recovered


def solution(mesh):
    return jax.shard_map(
        body,
        mesh=mesh,
        in_specs=(
            P("rows", "modes"),
            P("modes", "rows"),
            P("rows", "modes"),
            P(("rows", "modes"), None),
            P(),
            P(),
            P(),
        ),
        out_specs=P(("rows", "modes"), None),
        check_vma=False,
    )
```

profile of v0, /device:TPU:1, one launch (start us, length us, event | category | flops | bytes accessed | tf_op | source)
XLA Modules:
  0.0 808.9 jit_solution(13820839354043325952)
XLA Ops:
  7.3 4.0 multiply_reduce_fusion
  11.8 52.3 %all-gather.6.cloned.1.call-done = f32[256,1024]{1,0:T(8,128)} async-done(((f32[16,1024]{1,0:T(8,128)}), f32[256,1024]{1,0:T(8,128)}) %all-gather.6.cloned.1.call-update) | async-done | bytes 1048592 | tf_op jit(solution)/shard_map/all_gather | solution.py:82
  64.0 7.2 fusion.132
  71.5 60.0 %reduce-scatter.5.cloned.1.call-done = f32[16,1024]{1,0:T(8,128)} async-done(((f32[256,1024]{1,0:T(8,128)}), f32[16,1024]{1,0:T(8,128)}) %reduce-scatter.5.cloned.1.call-update) | async-done | bytes 65552 | tf_op jit(solution)/shard_map/reduce_scatter | solution.py:88
  131.5 1.5 sub.90
  133.2 65.1 %all-gather.8.cloned.1.call-done = f32[256,1024]{1,0:T(8,128)} async-done(((f32[16,1024]{1,0:T(8,128)}), f32[256,1024]{1,0:T(8,128)}) %all-gather.8.cloned.1.call-update) | async-done | bytes 1048592 | tf_op jit(solution)/shard_map/all_gather | solution.py:89
  198.3 7.2 fusion.133
  205.6 85.8 %psum.21 = f32[]{:T(128)} all-reduce(f32[]{:T(128)} %multiply_reduce_fusion), channel_id=1, replica_groups=mesh['rows'=16,'modes'=16] {'rows','modes'}, use_global_device_ids=true, to_apply=%region_1.0 | all-reduce | flops 1 | bytes 8 | tf_op jit(solution)/shard_map/psum | solution.py:77
  296.1 3.7 all-to-all-start
  301.3 33.4 %psum.22 = f32[256]{0:T(256)S(1)} all-reduce(f32[256]{0:T(256)S(1)} %multiply_reduce_fusion.2), channel_id=1, replica_groups=mesh['rows'=16,'modes'=16] {'rows'}, use_global_device_ids=true, to_apply=%region_5.0 | all-reduce | flops 256 | bytes 2048 | tf_op jit(solution)/shard_map/psum | solution.py:91
  339.5 1.7 fusion.26
  349.4 8.5 %convolution_bitcast_fusion.3 = f32[48,16384]{1,0:T(8,128)S(1)} fusion(bf16[48,432]{0,1:T(8,128)(2,1)S(1)} %bitcast.358, bf16[54,8,128,128]{3,2,1,0:T(8,128)(2,1)S(1)} %bitcast.352), kind=kOutput, calls=%fused_computation.3 | convolution fusion | flops 679477248 | bytes 17342976 | tf_op jit(solution)/shard_map/while/body/eval_jaxpr/dot_general | solution.py:43
  370.5 5.0 copy-done.6
  375.6 16.5 %fusion.16 = f32[16384,9]{0,1:T(8,128)} fusion(bf16[48,432]{0,1:T(8,128)(2,1)} %bitcast.359, bf16[54,8,128,128]{3,2,1,0:T(8,128)(2,1)} %bitcast.353, f32[48,16384]{1,0:T(8,128)} %copy-done.12, bf16[9,1,48]{2,0,1:T(8,128)(2,1)S(1)} %copy-done), kind=kOutput, calls=%fused_computation.50 | convolution fusion | flops 700710912 | bytes 17933664 | tf_op jit(solution)/shard_map/while/body/eval_jaxpr/dot_general | solution.py:17
  394.4 1.7 slice.508
  396.1 1.5 squeeze.169
  400.1 1.5 squeeze.165
  401.6 2.0 fusion.92
  404.3 1.7 multiply_reduce_fusion.5
  408.5 15.1 %all_to_all.45 = f32[1,16,1024]{2,0,1:T(1,128)} all-to-all(f32[1,16,1024]{2,0,1:T(1,128)S(1)} %fusion.114), channel_id=1, replica_groups=mesh['rows'=16,'modes'=16] {'modes'}, dimensions={1} | all-to-all | bytes 131072 | tf_op jit(solution)/shard_map/all_to_all | solution.py:114
  423.9 47.2 %all-gather.12.cloned.1.call-done = f32[1,256,1024]{2,0,1:T(1,128)} async-done(((f32[1,16,1024]{2,0,1:T(1,128)}), f32[1,256,1024]{2,0,1:T(1,128)}) %all-gather.12.cloned.1.call-update) | async-done | bytes 1048592 | tf_op jit(solution)/shard_map/all_gather | solution.py:82
  471.0 7.2 fusion.77
  478.3 60.2 %reduce-scatter.9.cloned.1.call-done = f32[16,1024]{1,0:T(8,128)} async-done(((f32[256,1024]{1,0:T(8,128)}), f32[16,1024]{1,0:T(8,128)}) %reduce-scatter.9.cloned.1.call-update) | async-done | bytes 65552 | tf_op jit(solution)/shard_map/reduce_scatter | solution.py:88
  538.5 1.5 sub.98
  540.0 65.2 %all-gather.10.cloned.1.call-done = f32[256,1024]{1,0:T(8,128)} async-done(((f32[16,1024]{1,0:T(8,128)}), f32[256,1024]{1,0:T(8,128)}) %all-gather.10.cloned.1.call-update) | async-done | bytes 1048592 | tf_op jit(solution)/shard_map/all_gather | solution.py:89
  605.2 7.2 fusion.134
  612.5 81.3 %reduce-scatter.11.cloned.1.call-done = f32[16,1024]{1,0:T(8,128)} async-done(((f32[256,1024]{1,0:T(8,128)}), f32[16,1024]{1,0:T(8,128)}) %reduce-scatter.11.cloned.1.call-update) | async-done | bytes 65552 | tf_op jit(solution)/shard_map/reduce_scatter | solution.py:93
  695.3 7.3 all-to-all-start.2
  703.9 35.5 %psum.23 = f32[256]{0:T(256)S(1)} all-reduce(f32[256]{0:T(256)S(1)} %multiply_reduce_fusion.1), channel_id=1, replica_groups=mesh['rows'=16,'modes'=16] {'rows'}, use_global_device_ids=true, to_apply=%region_12.13 | all-reduce | flops 256 | bytes 2048 | tf_op jit(solution)/shard_map/psum | solution.py:91
  753.8 8.7 %convolution_bitcast_fusion.1 = f32[48,16384]{1,0:T(8,128)S(1)} fusion(bf16[48,432]{0,1:T(8,128)(2,1)S(1)} %bitcast.360, bf16[54,8,128,128]{3,2,1,0:T(8,128)(2,1)S(1)} %bitcast.354), kind=kOutput, calls=%fused_computation.1 | convolution fusion | flops 679477248 | bytes 17342976 | tf_op jit(solution)/shard_map/while/body/eval_jaxpr/dot_general | solution.py:43
  773.0 5.0 copy-done.7
  778.1 16.5 %fusion.13 = f32[16384,9]{0,1:T(8,128)} fusion(bf16[48,432]{0,1:T(8,128)(2,1)S(1)} %bitcast.361, bf16[54,8,128,128]{3,2,1,0:T(8,128)(2,1)} %bitcast.355, f32[48,16384]{1,0:T(8,128)} %copy-done.13, bf16[9,1,48]{2,0,1:T(8,128)(2,1)S(1)} %copy-done), kind=kOutput, calls=%fused_computation.49 | convolution fusion | flops 700710912 | bytes 17933664 | tf_op jit(solution)/shard_map/while/body/eval_jaxpr/dot_general | solution.py:17
  (162 shorter events, 68.6 us)
Async XLA Ops:
  6.5 351.4 %copy-start = (bf16[9,1,48]{2,0,1:T(8,128)(2,1)S(1)}, bf16[9,1,48]{2,0,1:T(8,128)(2,1)}, u32[]{:S(2)}) copy-start(bf16[9,1,48]{2,0,1:T(8,128)(2,1)} %param.13) | copy-start | bytes 2596
  6.5 4.7 copy-start.4
  6.5 57.5 %all-gather.6.cloned.1.call-start = ((), (), s32[]{:S(2)}) async-start(), calls=%async_computation.7 | async-start | bytes 1114112 | tf_op jit(solution)/shard_map/all_gather | solution.py:82
  7.3 124.2 %reduce-scatter.5.cloned.1.call-start = ((), (), s32[]{:S(2)}) async-start(), calls=%async_computation.8 | async-start | bytes 1114112 | tf_op jit(solution)/shard_map/reduce_scatter | solution.py:88
  11.7 119.7 %copy-start.2 = (f32[16,1024]{1,0:T(8,128)S(1)}, f32[16,1024]{1,0:T(8,128)}, u32[]{:S(2)}) copy-start(f32[16,1024]{1,0:T(8,128)} %param.8) | copy-start | bytes 196612
  71.3 127.0 %all-gather.8.cloned.1.call-start = ((), (), s32[]{:S(2)}) async-start(), calls=%async_computation.9 | async-start | bytes 1114112 | tf_op jit(solution)/shard_map/all_gather | solution.py:89
  133.0 161.5 %reduce-scatter.7.cloned.1.call-start = ((), (), s32[]{:S(2)}) async-start(), calls=%async_computation.10 | async-start | bytes 1114112 | tf_op jit(solution)/shard_map/reduce_scatter | solution.py:93
  133.1 158.3 %copy-start.8 = (bf16[9,48,48]{2,1,0:T(8,128)(2,1)S(1)}, bf16[9,48,48]{2,1,0:T(8,128)(2,1)}, u32[]{:S(2)}) copy-start(bf16[9,48,48]{2,1,0:T(8,128)(2,1)} %param.12) | copy-start | bytes 124420
  133.1 159.4 %copy-start.11 = (bf16[9,48,2]{1,2,0:T(2,128)(2,1)S(1)}, bf16[9,48,2]{1,2,0:T(2,128)(2,1)}, u32[]{:S(2)}) copy-start(bf16[9,48,2]{1,2,0:T(2,128)(2,1)} %param.11) | copy-start | bytes 5188
  291.6 57.8 %copy-start.9 = (bf16[48,9,48]{0,2,1:T(8,128)(2,1)}, bf16[48,9,48]{0,2,1:T(8,128)(2,1)S(1)}, u32[]{:S(2)}) copy-start(bf16[48,9,48]{0,2,1:T(8,128)(2,1)S(1)} %copy.21) | copy-start | bytes 124420
  293.2 1.4 copy-start.5
  296.1 40.7 %all-to-all-start = ((f32[16,1,1024]{2,1,0:T(1,128)}), f32[16,1,1024]{2,1,0:T(1,128)S(1)}, u32[]{:S(2)}, u32[]{:S(2)}) async-start(f32[16,1,1024]{2,1,0:T(1,128)} %copy.20), calls=%async_computation.2 | async-start | bytes 131072 | tf_op jit(solution)/shard_map/all_to_all | solution.py:105
  299.8 171.2 %all-gather.12.cloned.1.call-start = ((), (), s32[]{:S(2)}) async-start(), calls=%async_computation.14 | async-start | bytes 1114112 | tf_op jit(solution)/shard_map/all_gather | solution.py:82
  357.9 1.6 copy-start.12
  370.5 5.1 copy-start.6
  423.6 114.9 %copy-start.3 = (f32[16,1024]{1,0:T(8,128)S(1)}, f32[16,1024]{1,0:T(8,128)}, u32[]{:S(2)}) copy-start(f32[16,1024]{1,0:T(8,128)} %param.8) | copy-start | bytes 196612
  423.6 114.8 %reduce-scatter.9.cloned.1.call-start = ((), (), s32[]{:S(2)}) async-start(), calls=%async_computation.11 | async-start | bytes 1114112 | tf_op jit(solution)/shard_map/reduce_scatter | solution.py:88
  478.3 127.0 %all-gather.10.cloned.1.call-start = ((), (), s32[]{:S(2)}) async-start(), calls=%async_computation.12 | async-start | bytes 1114112 | tf_op jit(solution)/shard_map/all_gather | solution.py:89
  540.0 153.7 %copy-start.1 = (f32[1,16,1024]{2,0,1:T(1,128)S(1)}, f32[1,16,1024]{2,0,1:T(1,128)}, u32[]{:S(2)}) copy-start(f32[1,16,1024]{2,0,1:T(1,128)} %all_to_all.45) | copy-start | bytes 196612
  540.0 153.7 %reduce-scatter.11.cloned.1.call-start = ((), (), s32[]{:S(2)}) async-start(), calls=%async_computation.13 | async-start | bytes 1114112 | tf_op jit(solution)/shard_map/reduce_scatter | solution.py:93
  695.3 46.1 %all-to-all-start.2 = ((f32[16,1,1024]{2,1,0:T(1,128)}), f32[16,1,1024]{2,1,0:T(1,128)S(1)}, u32[]{:S(2)}, u32[]{:S(2)}) async-start(f32[16,1,1024]{2,1,0:T(1,128)} %copy.24), calls=%async_computation.6 | async-start | bytes 131072 | tf_op jit(solution)/shard_map/all_to_all | solution.py:105
  751.7 2.1 copy-start.10
  762.6 1.6 copy-start.13
  773.0 5.1 copy-start.7
Sparse Core Ops, SparseCore 0:
  10.1 53.9 all-gather.5
  71.4 59.9 reduce-scatter.4
  133.3 64.9 all-gather.7
  205.6 81.1 reduce-scatter.6
  423.7 47.2 all-gather.11
  478.4 60.0 reduce-scatter.8
  540.3 64.9 all-gather.9
  612.6 81.0 reduce-scatter.10
where the time goes:
time: 818 us; the launch traced here: 809 us
  waiting for transfers between devices  432 us (53%)
  blocking collectives  170 us (21%)
  matrix products  82.9 us (10%)
  local copies, waits for them, and re-layouts  67.3 us (8%)
  other arithmetic  23.2 us (3%)
  between operations  22 us (3%)
  starting transfers between devices  11.5 us (1%)
    all_gather x2, waiting for transfers between devices, body(): misfit_all = lax.all_gather(observed - fitted, 'modes', axis=0, tiled=True)  130 us
    reduce_scatter x2, waiting for transfers between devices, body(): lax.psum_scatter(partial_value, 'modes', scatter_dimension=0, tiled=True)  120 us
    all_gather x2, waiting for transfers between devices, body(): lax.all_gather(estimate, 'rows', axis=0, tiled=True)  99.5 us
    psum x1, blocking collectives, body(): trace = lax.psum(jnp.sum(transfer * transfer), ('rows', 'modes'))  85.8 us
    reduce_scatter x2, waiting for transfers between devices, body(): lax.psum_scatter(jnp.dot(misfit_all, transfer, precision=lax.Precision.HI...  81.3 us
    psum x2, blocking collectives, body(): squares_all = lax.psum(square_part[:, 0], 'rows')  68.9 us
    unnamed x88, local copies, waits for them, and re-layouts  46.9 us
    dot_general x4, matrix products, conv_layer(): jnp.dot(taps_flat, feature.reshape(in_chan, extent_rows * extent_cols), p...  35 us
  transfers between devices with their start and end apart: 10, of which 7 were waited for; matrix products, arithmetic and copies ran while one was open for 1% of the time, Pallas kernels for 0%

commit v1 on v0

--- a/solution.py
+++ b/solution.py
@@ -86,7 +86,10 @@
             preferred_element_type=jnp.float32,
         )
         fitted = lax.psum_scatter(partial_value, "modes", scatter_dimension=0, tiled=True)
-        misfit_all = lax.all_gather(observed - fitted, "modes", axis=0, tiled=True)
+        misfit_all = jnp.concatenate(
+            lax.all_to_all(jnp.stack([observed - fitted] * lax.axis_size("modes")), "modes", 0, 0),
+            axis=0,
+        )
         square_part = jnp.sum(misfit_all * misfit_all, axis=1, keepdims=True)
         squares_all = lax.psum(square_part[:, 0], "rows")
         squares = lax.dynamic_slice_in_dim(squares_all, offset_frame, frames_dev)

time: 818 us -> 732 us (0.89)
  waiting for transfers between devices: 432 us -> 320 us
  blocking collectives: 170 us -> 190 us
    all_gather x2 -> x0, waiting for transfers between devices: 130 us -> none  [body(): misfit_all = lax.all_gather(observed - fitted, 'modes', axis=0, tiled=True)]
    all_to_all x0 -> x1, blocking collectives: none -> 18.2 us  [body(): lax.all_to_all(jnp.stack([observed - fitted] * lax.axis_size('modes')), '...]
    all_to_all x0 -> x1, waiting for transfers between devices: none -> 15.7 us  [body(): lax.all_to_all(jnp.stack([observed - fitted] * lax.axis_size('modes')), '...]
    unnamed x88 -> x92, local copies, waits for them, and re-layouts: 46.9 us -> 47.8 us
  transfers between devices with their start and end apart: 10 -> 9, of which waited for: 7 -> 6; matrix products, arithmetic and copies ran while one was open for 1% -> 2% of each run, Pallas kernels for 0% -> 0%
where the time goes in v1:
time: 732 us; the launch traced here: 722 us
  waiting for transfers between devices  320 us (44%)
  blocking collectives  190 us (26%)
  matrix products  82.4 us (11%)
  local copies, waits for them, and re-layouts  69.6 us (10%)
  between operations  22.3 us (3%)
  other arithmetic  21.9 us (3%)
  starting transfers between devices  16.2 us (2%)
    reduce_scatter x2, waiting for transfers between devices, body(): lax.psum_scatter(partial_value, 'modes', scatter_dimension=0, tiled=True)  120 us
    all_gather x2, waiting for transfers between devices, body(): lax.all_gather(estimate, 'rows', axis=0, tiled=True)  98.9 us
    psum x1, blocking collectives, body(): trace = lax.psum(jnp.sum(transfer * transfer), ('rows', 'modes'))  87.1 us
    reduce_scatter x2, waiting for transfers between devices, body(): lax.psum_scatter(jnp.dot(misfit_all, transfer, precision=lax.Precision.HI...  84.8 us
    psum x2, blocking collectives, body(): squares_all = lax.psum(square_part[:, 0], 'rows')  69.2 us
    unnamed x92, local copies, waits for them, and re-layouts  47.8 us
    dot_general x4, matrix products, conv_layer(): jnp.dot(taps_flat, feature.reshape(in_chan, extent_rows * extent_cols), p...  35 us
    dot_general x5, matrix products, conv_layer(): summed = jnp.dot(weight_flat, columns, preferred_element_type=jnp.float32)  18.8 us
  transfers between devices with their start and end apart: 9, of which 6 were waited for; matrix products, arithmetic and copies ran while one was open for 2% of the time, Pallas kernels for 0%

profile of v1, /device:TPU:1, one launch (start us, length us, event | category | flops | bytes accessed | tf_op | source)
XLA Modules:
  0.0 722.3 jit_solution(12578322446742217130)
XLA Ops:
  7.3 3.9 multiply_reduce_fusion
  11.7 52.4 %all-gather.4.cloned.1.call-done = f32[256,1024]{1,0:T(8,128)} async-done(((f32[16,1024]{1,0:T(8,128)}), f32[256,1024]{1,0:T(8,128)}) %all-gather.4.cloned.1.call-update) | async-done | bytes 1048592 | tf_op jit(solution)/shard_map/all_gather | solution.py:82
  64.0 7.2 fusion.132
  71.4 60.0 %reduce-scatter.5.cloned.1.call-done = f32[16,1024]{1,0:T(8,128)} async-done(((f32[256,1024]{1,0:T(8,128)}), f32[16,1024]{1,0:T(8,128)}) %reduce-scatter.5.cloned.1.call-update) | async-done | bytes 65552 | tf_op jit(solution)/shard_map/reduce_scatter | solution.py:88
  133.4 3.7 all-to-all-start
  137.2 15.7 %all-to-all-done = f32[16,16,1024]{2,1,0:T(8,128)S(1)} async-done(((f32[16,16,1024]{2,1,0:T(8,128)}), f32[16,16,1024]{2,1,0:T(8,128)S(1)}, u32[]{:S(2)}, u32[]{:S(2)}) %all-to-all-start) | async-done | bytes 1048608 | tf_op jit(solution)/shard_map/all_to_all | solution.py:90
  152.8 7.3 %fusion.133 = f32[256,1024]{1,0:T(8,128)} fusion(f32[256,1024]{1,0:T(8,128)S(1)} %bitcast.321, f32[1024,1024]{1,0:T(8,128)} %param.7), kind=kOutput, calls=%fused_computation.290 | convolution fusion | flops 3221225472 | bytes 6291456 | tf_op jit(solution)/shard_map/dot_general | solution.py:97
  160.3 87.1 %psum.21 = f32[]{:T(128)} all-reduce(f32[]{:T(128)} %multiply_reduce_fusion), channel_id=1, replica_groups=mesh['rows'=16,'modes'=16] {'rows','modes'}, use_global_device_ids=true, to_apply=%region_1.0 | all-reduce | flops 1 | bytes 8 | tf_op jit(solution)/shard_map/psum | solution.py:77
  252.1 4.6 all-to-all-start.1
  258.2 33.9 %psum.22 = f32[256]{0:T(256)S(1)} all-reduce(f32[256]{0:T(256)S(1)} %reduce_sum.89), channel_id=1, replica_groups=mesh['rows'=16,'modes'=16] {'rows'}, use_global_device_ids=true, to_apply=%region_5.0 | all-reduce | flops 256 | bytes 2048 | tf_op jit(solution)/shard_map/psum | solution.py:94
  296.8 1.7 fusion.26
  306.7 8.5 %convolution_bitcast_fusion.3 = f32[48,16384]{1,0:T(8,128)S(1)} fusion(bf16[48,432]{0,1:T(8,128)(2,1)S(1)} %bitcast.362, bf16[54,8,128,128]{3,2,1,0:T(8,128)(2,1)S(1)} %bitcast.356), kind=kOutput, calls=%fused_computation.3 | convolution fusion | flops 679477248 | bytes 17342976 | tf_op jit(solution)/shard_map/while/body/eval_jaxpr/dot_general | solution.py:43
  327.7 5.0 copy-done.8
  332.7 16.6 %fusion.16 = f32[16384,9]{0,1:T(8,128)} fusion(bf16[48,432]{0,1:T(8,128)(2,1)} %bitcast.363, bf16[54,8,128,128]{3,2,1,0:T(8,128)(2,1)} %bitcast.357, f32[48,16384]{1,0:T(8,128)} %copy-done.14, bf16[9,1,48]{2,0,1:T(8,128)(2,1)S(1)} %copy-done), kind=kOutput, calls=%fused_computation.50 | convolution fusion | flops 700710912 | bytes 17933664 | tf_op jit(solution)/shard_map/while/body/eval_jaxpr/dot_general | solution.py:17
  351.5 1.7 slice.508
  353.3 1.5 squeeze.169
  357.3 1.5 squeeze.165
  358.8 2.0 fusion.92
  361.4 1.7 multiply_reduce_fusion.5
  365.6 15.1 %all_to_all.55 = f32[1,16,1024]{2,0,1:T(1,128)} all-to-all(f32[1,16,1024]{2,0,1:T(1,128)S(1)} %fusion.114), channel_id=1, replica_groups=mesh['rows'=16,'modes'=16] {'modes'}, dimensions={1} | all-to-all | bytes 131072 | tf_op jit(solution)/shard_map/all_to_all | solution.py:117
  381.2 46.6 %all-gather.6.cloned.1.call-done = f32[1,256,1024]{2,0,1:T(1,128)} async-done(((f32[1,16,1024]{2,0,1:T(1,128)}), f32[1,256,1024]{2,0,1:T(1,128)}) %all-gather.6.cloned.1.call-update) | async-done | bytes 1048592 | tf_op jit(solution)/shard_map/all_gather | solution.py:82
  427.8 7.2 fusion.77
  435.0 60.1 %reduce-scatter.9.cloned.1.call-done = f32[16,1024]{1,0:T(8,128)} async-done(((f32[256,1024]{1,0:T(8,128)}), f32[16,1024]{1,0:T(8,128)}) %reduce-scatter.9.cloned.1.call-update) | async-done | bytes 65552 | tf_op jit(solution)/shard_map/reduce_scatter | solution.py:88
  496.1 18.2 %all_to_all.56 = f32[16,16,1024]{2,1,0:T(8,128)S(1)} all-to-all(f32[16,16,1024]{2,1,0:T(8,128)S(1)} %stack.14), channel_id=1, replica_groups=mesh['rows'=16,'modes'=16] {'modes'}, dimensions={0} | all-to-all | bytes 2097152 | tf_op jit(solution)/shard_map/all_to_all | solution.py:90
  515.3 6.9 fusion.134
  522.2 84.7 %reduce-scatter.11.cloned.1.call-done = f32[16,1024]{1,0:T(8,128)} async-done(((f32[256,1024]{1,0:T(8,128)}), f32[16,1024]{1,0:T(8,128)}) %reduce-scatter.11.cloned.1.call-update) | async-done | bytes 65552 | tf_op jit(solution)/shard_map/reduce_scatter | solution.py:96
  608.5 7.3 %all-to-all-start.4 = ((f32[16,1,1024]{2,1,0:T(1,128)}), f32[16,1,1024]{2,1,0:T(1,128)S(1)}, u32[]{:S(2)}, u32[]{:S(2)}) async-start(f32[16,1,1024]{2,1,0:T(1,128)} %copy.29), calls=%async_computation.8 | async-start | bytes 131072 | tf_op jit(solution)/shard_map/all_to_all | solution.py:108
  617.3 35.3 %psum.23 = f32[256]{0:T(256)S(1)} all-reduce(f32[256]{0:T(256)S(1)} %reduce_sum.94), channel_id=1, replica_groups=mesh['rows'=16,'modes'=16] {'rows'}, use_global_device_ids=true, to_apply=%region_12.13 | all-reduce | flops 256 | bytes 2048 | tf_op jit(solution)/shard_map/psum | solution.py:94
  667.1 8.5 %convolution_bitcast_fusion.1 = f32[48,16384]{1,0:T(8,128)S(1)} fusion(bf16[48,432]{0,1:T(8,128)(2,1)S(1)} %bitcast.364, bf16[54,8,128,128]{3,2,1,0:T(8,128)(2,1)S(1)} %bitcast.358), kind=kOutput, calls=%fused_computation.1 | convolution fusion | flops 679477248 | bytes 17342976 | tf_op jit(solution)/shard_map/while/body/eval_jaxpr/dot_general | solution.py:43
  682.5 1.5 fusion.70
  686.1 5.0 copy-done.9
  691.2 16.5 %fusion.13 = f32[16384,9]{0,1:T(8,128)} fusion(bf16[48,432]{0,1:T(8,128)(2,1)S(1)} %bitcast.365, bf16[54,8,128,128]{3,2,1,0:T(8,128)(2,1)} %bitcast.359, f32[48,16384]{1,0:T(8,128)} %copy-done.15, bf16[9,1,48]{2,0,1:T(8,128)(2,1)S(1)} %copy-done), kind=kOutput, calls=%fused_computation.49 | convolution fusion | flops 700710912 | bytes 17933664 | tf_op jit(solution)/shard_map/while/body/eval_jaxpr/dot_general | solution.py:17
  (167 shorter events, 71.1 us)
Async XLA Ops:
  6.5 308.7 %copy-start = (bf16[9,1,48]{2,0,1:T(8,128)(2,1)S(1)}, bf16[9,1,48]{2,0,1:T(8,128)(2,1)}, u32[]{:S(2)}) copy-start(bf16[9,1,48]{2,0,1:T(8,128)(2,1)} %param.13) | copy-start | bytes 2596
  6.5 4.6 copy-start.6
  6.5 57.5 %all-gather.4.cloned.1.call-start = ((), (), s32[]{:S(2)}) async-start(), calls=%async_computation.9 | async-start | bytes 1114112 | tf_op jit(solution)/shard_map/all_gather | solution.py:82
  7.3 124.1 %reduce-scatter.5.cloned.1.call-start = ((), (), s32[]{:S(2)}) async-start(), calls=%async_computation.10 | async-start | bytes 1114112 | tf_op jit(solution)/shard_map/reduce_scatter | solution.py:88
  11.7 119.7 %copy-start.4 = (f32[16,1024]{1,0:T(8,128)S(1)}, f32[16,1024]{1,0:T(8,128)}, u32[]{:S(2)}) copy-start(f32[16,1024]{1,0:T(8,128)} %param.8) | copy-start | bytes 196612
  133.4 19.5 %all-to-all-start = ((f32[16,16,1024]{2,1,0:T(8,128)}), f32[16,16,1024]{2,1,0:T(8,128)S(1)}, u32[]{:S(2)}, u32[]{:S(2)}) async-start(f32[16,16,1024]{2,1,0:T(8,128)} %stack.12), calls=%async_computation.1 | async-start | bytes 2097152 | tf_op jit(solution)/shard_map/all_to_all | solution.py:90
  137.0 113.5 %reduce-scatter.7.cloned.1.call-start = ((), (), s32[]{:S(2)}) async-start(), calls=%async_computation.11 | async-start | bytes 1114112 | tf_op jit(solution)/shard_map/reduce_scatter | solution.py:96
  152.8 7.3 %copy-start.1 = (f32[16,16,1024]{2,1,0:T(8,128)}, f32[16,16,1024]{2,1,0:T(8,128)S(1)}, u32[]{:S(2)}) copy-start(f32[16,16,1024]{2,1,0:T(8,128)S(1)} %all-to-all-done) | copy-start | bytes 3145732
  152.8 94.6 %copy-start.10 = (bf16[9,48,48]{2,1,0:T(8,128)(2,1)S(1)}, bf16[9,48,48]{2,1,0:T(8,128)(2,1)}, u32[]{:S(2)}) copy-start(bf16[9,48,48]{2,1,0:T(8,128)(2,1)} %param.12) | copy-start | bytes 124420
  152.8 95.7 %copy-start.13 = (bf16[9,48,2]{1,2,0:T(2,128)(2,1)S(1)}, bf16[9,48,2]{1,2,0:T(2,128)(2,1)}, u32[]{:S(2)}) copy-start(bf16[9,48,2]{1,2,0:T(2,128)(2,1)} %param.11) | copy-start | bytes 5188
  247.6 59.2 %copy-start.11 = (bf16[48,9,48]{0,2,1:T(8,128)(2,1)}, bf16[48,9,48]{0,2,1:T(8,128)(2,1)S(1)}, u32[]{:S(2)}) copy-start(bf16[48,9,48]{0,2,1:T(8,128)(2,1)S(1)} %copy.26) | copy-start | bytes 124420
  249.1 1.4 copy-start.7
  252.1 42.1 %all-to-all-start.1 = ((f32[16,1,1024]{2,1,0:T(1,128)}), f32[16,1,1024]{2,1,0:T(1,128)S(1)}, u32[]{:S(2)}, u32[]{:S(2)}) async-start(f32[16,1,1024]{2,1,0:T(1,128)} %copy.25), calls=%async_computation.3 | async-start | bytes 131072 | tf_op jit(solution)/shard_map/all_to_all | solution.py:108
  256.7 171.1 %all-gather.6.cloned.1.call-start = ((), (), s32[]{:S(2)}) async-start(), calls=%async_computation.14 | async-start | bytes 1114112 | tf_op jit(solution)/shard_map/all_gather | solution.py:82
  315.2 1.6 copy-start.14
  327.7 5.1 copy-start.8
  380.7 114.4 %copy-start.5 = (f32[16,1024]{1,0:T(8,128)S(1)}, f32[16,1024]{1,0:T(8,128)}, u32[]{:S(2)}) copy-start(f32[16,1024]{1,0:T(8,128)} %param.8) | copy-start | bytes 196612
  380.8 114.4 %reduce-scatter.9.cloned.1.call-start = ((), (), s32[]{:S(2)}) async-start(), calls=%async_computation.12 | async-start | bytes 1114112 | tf_op jit(solution)/shard_map/reduce_scatter | solution.py:88
  435.0 172.0 %reduce-scatter.11.cloned.1.call-start = ((), (), s32[]{:S(2)}) async-start(), calls=%async_computation.13 | async-start | bytes 1114112 | tf_op jit(solution)/shard_map/reduce_scatter | solution.py:96
  514.3 1.0 copy-start.2
  515.3 91.7 %copy-start.3 = (f32[1,16,1024]{2,0,1:T(1,128)S(1)}, f32[1,16,1024]{2,0,1:T(1,128)}, u32[]{:S(2)}) copy-start(f32[1,16,1024]{2,0,1:T(1,128)} %all_to_all.55) | copy-start | bytes 196612
  608.5 46.1 %all-to-all-start.4 = ((f32[16,1,1024]{2,1,0:T(1,128)}), f32[16,1,1024]{2,1,0:T(1,128)S(1)}, u32[]{:S(2)}, u32[]{:S(2)}) async-start(f32[16,1,1024]{2,1,0:T(1,128)} %copy.29), calls=%async_computation.8 | async-start | bytes 131072 | tf_op jit(solution)/shard_map/all_to_all | solution.py:108
  665.0 2.1 copy-start.12
  675.6 1.6 copy-start.15
  686.1 5.1 copy-start.9
Sparse Core Ops, SparseCore 0:
  10.1 53.9 all-gather.3
  71.4 59.9 reduce-scatter.4
  160.3 82.4 reduce-scatter.6
  380.9 46.8 all-gather.5
  435.1 59.9 reduce-scatter.8
  522.3 84.5 reduce-scatter.10
